TPU v7x, 512 devices: a whole 4x8x8 slice. The times are simulated.
512 devices in a mesh: row: 16 (over z, x_lo), col: 32 (over x_hi, y, core).
Axes of the slice: x: 4 (x_hi: 2, x_lo: 2; x = x_hi * 2 + x_lo), y: 8, z: 8, core: 2. Of those that a mesh axis runs over, the one named last changes fastest.
Arguments:
- tokens: bfloat16 [2048, 4096], P('row', 'col'), may hold values from -6 to 6
- upstream: bfloat16 [2048, 4096], P('row', 'col'), may hold values from -6 to 6
- w_in: bfloat16 [32, 16, 256, 256], P('col', 'row'), may hold values from -0.1875 to 0.1875
- in_codes: int32 [32, 16], P('col'), may hold values from -1 to 31, as said below
- w_out: bfloat16 [32, 16, 256, 256], P('col', 'row'), may hold values from -0.09375 to 0.09375
- out_codes: int32 [32, 16], P('col'), may hold values from -1 to 31, as said below
Outputs:
- layer_out: bfloat16 [2048, 4096], P('row', 'col')
- grad_tokens: bfloat16 [2048, 4096], P('row', 'col')
- grad_w_in: bfloat16 [32, 16, 256, 256], P('col', 'row')
- grad_w_out: bfloat16 [32, 16, 256, 256], P('col', 'row')
Inputs may be any that keep to these rules, and one draw needn't show every extreme that they name: `in_codes`: row c describes panel c's 16 slots: a code k names input tile row k // 2 and local hidden tile column k % 2; -1 marks an empty slot. Codes of a row are distinct, every row has one filled slot or more, and some row has all 16 slots filled. `out_codes`: row c describes panel c's 16 slots: a code k names output tile column k // 2 and local hidden tile row k % 2; -1 marks an empty slot. Codes of a row are distinct, every row has one filled slot or more, and some row has all 16 slots filled.
All inputs are finite; a program needn't handle non-finite values.
Results may differ from a plain program's by a relative error of at most 0.015.
Values may be sent and summed in bfloat16 or wider, within the bound.
A program may use at most 64 MiB of HBM per device.

v0:
```python
import jax
import jax.numpy as jnp
from jax import lax
from jax.sharding import PartitionSpec as P

D = 4096
FF = 16384


def silu_slope(hidden):
    sigmoid_value = jax.nn.sigmoid(hidden)
    return sigmoid_value * (1.0 + hidden * (1.0 - sigmoid_value))


def split_codes(slot_codes, tile_cols):
    filled = slot_codes >= 0
    clipped = jnp.maximum(slot_codes, 0)
    return (clipped // tile_cols, clipped % tile_cols, filled)


def selector(position, filled, classes):
    matches = position[:, None] == jnp.arange(classes, dtype=jnp.int32)[None, :]
    return (matches & filled[:, None]).astype(jnp.float32)


def slices_at(row_codes, col_codes, filled):
    return (row_codes, col_codes, filled)


def per_device(tokens, upstream, w_in, in_codes, w_out, out_codes):
    tile_size = w_in.shape[3]
    row_count = tokens.shape[0]
    tile_rows = D // tile_size
    tile_cols = FF // (tile_size * lax.axis_size("col"))
    own_slots = w_in.shape[1]
    highest = lax.Precision.HIGHEST
    in_row, in_col, in_filled = split_codes(in_codes[0], tile_cols)
    out_row, out_col, out_filled = split_codes(out_codes[0], tile_cols)
    first_slot = lax.axis_index("row") * own_slots
    whole_tokens, whole_upstream = (
        lax.all_gather(tokens, "col", axis=1, tiled=True),
        lax.all_gather(upstream, "col", axis=1, tiled=True),
    )
    token_tiles = whole_tokens.reshape(row_count, tile_rows, tile_size)
    up_tiles = whole_upstream.reshape(row_count, tile_rows, tile_size)
    slot_major_tokens = jnp.swapaxes(token_tiles, 0, 1)
    rows_at, cols_at, filled_at = slices_at(in_row, in_col, in_filled)
    picked = jnp.take(token_tiles, rows_at, axis=1)
    partial_sum = jnp.einsum(
        "tkd,kdn->tkn",
        picked,
        lax.all_gather(w_in, "row", axis=1, tiled=True)[0],
        preferred_element_type=jnp.float32,
    )
    hidden = jnp.einsum(
        "tkn,kj->tjn", partial_sum, selector(cols_at, filled_at, tile_cols), precision=highest
    )
    activ = jax.nn.silu(hidden).astype(jnp.bfloat16)
    rows_at, cols_at, filled_at = slices_at(out_row, out_col, out_filled)
    picked = jnp.take(activ, cols_at, axis=1)
    partial_sum = jnp.einsum(
        "tkf,kfd->tkd",
        picked,
        lax.all_gather(w_out, "row", axis=1, tiled=True)[0],
        preferred_element_type=jnp.float32,
    )
    layer_part = jnp.einsum(
        "tkd,ki->tid", partial_sum, selector(rows_at, filled_at, tile_rows), precision=highest
    )
    layer_out = lax.psum_scatter(
        layer_part.reshape(row_count, D).astype(jnp.bfloat16),
        "col",
        scatter_dimension=1,
        tiled=True,
    )
    rows_at, cols_at, filled_at = slices_at(out_row, out_col, out_filled)
    picked = jnp.take(up_tiles, rows_at, axis=1)
    partial_sum = jnp.einsum(
        "tkd,kfd->tkf",
        picked,
        lax.all_gather(w_out, "row", axis=1, tiled=True)[0],
        preferred_element_type=jnp.float32,
    )
    grad_activ = jnp.einsum(
        "tkf,kj->tjf", partial_sum, selector(cols_at, filled_at, tile_cols), precision=highest
    )
    grad_hidden = (grad_activ * silu_slope(hidden)).astype(jnp.bfloat16)
    grad_sends = jnp.take(jnp.swapaxes(grad_hidden, 0, 1), in_col, axis=0)
    activ_sends = jnp.take(jnp.swapaxes(activ, 0, 1), out_col, axis=0)
    upstream_sends = jnp.take(jnp.swapaxes(up_tiles, 0, 1), out_row, axis=0)
    token_sends = jnp.take(slot_major_tokens, in_row, axis=0)
    token_slots, grad_slots, activ_slots, upstream_slots = (
        lax.all_to_all(token_sends, "row", split_axis=0, concat_axis=1, tiled=True),
        lax.all_to_all(grad_sends, "row", split_axis=0, concat_axis=1, tiled=True),
        lax.all_to_all(activ_sends, "row", split_axis=0, concat_axis=1, tiled=True),
        lax.all_to_all(upstream_sends, "row", split_axis=0, concat_axis=1, tiled=True),
    )
    rows_at, cols_at, filled_at = slices_at(in_row, in_col, in_filled)
    picked = jnp.take(grad_hidden, cols_at, axis=1)
    partial_sum = jnp.einsum(
        "tkf,kdf->tkd",
        picked,
        lax.all_gather(w_in, "row", axis=1, tiled=True)[0],
        preferred_element_type=jnp.float32,
    )
    input_part = jnp.einsum(
        "tkd,ki->tid", partial_sum, selector(rows_at, filled_at, tile_rows), precision=highest
    )
    grad_tokens = lax.psum_scatter(
        input_part.reshape(row_count, D).astype(jnp.bfloat16),
        "col",
        scatter_dimension=1,
        tiled=True,
    )
    mine_in = lax.dynamic_slice_in_dim(in_filled, first_slot, own_slots)
    mine_out = lax.dynamic_slice_in_dim(out_filled, first_slot, own_slots)
    grad_w_in = jnp.einsum(
        "ktd,ktn->kdn", token_slots, grad_slots, preferred_element_type=jnp.float32
    )
    grad_w_in = jnp.where(mine_in[:, None, None], grad_w_in, 0.0).astype(jnp.bfloat16)[None]
    grad_w_out = jnp.einsum(
        "ktf,ktd->kfd", activ_slots, upstream_slots, preferred_element_type=jnp.float32
    )
    grad_w_out = jnp.where(mine_out[:, None, None], grad_w_out, 0.0).astype(jnp.bfloat16)[None]
    return (layer_out, grad_tokens, grad_w_in, grad_w_out)


def solution(mesh):
    placed = (
        P("row", "col"),
        P("row", "col"),
        P("col", "row", None, None),
        P("col", None),
        P("col", "row", None, None),
        P("col", None),
    )
    return jax.shard_map(
        per_device,
        mesh=mesh,
        in_specs=placed,
        out_specs=(
            P("row", "col"),
            P("row", "col"),
            P("col", "row", None, None),
            P("col", "row", None, None),
        ),
        check_vma=False,
    )
```

profile of v0, /device:TPU:16, one launch (start us, length us, event | category | flops | bytes accessed | tf_op | source)
XLA Modules:
  0.0 631.0 jit_solution(14606275297330410834)
XLA Ops:
  7.2 0.0 all-gather.11.cloned.1.call-start
  7.2 1.5 copy.59
  8.7 0.0 all-gather.11.cloned.1.call-update
  8.7 0.0 all-gather.5.cloned.1.call-start
  8.8 1.5 copy.52
  10.2 0.0 all-gather.5.cloned.1.call-update
  10.3 0.0 all-gather.9.cloned.1.call-start
  10.3 0.7 all-gather.9.cloned.1.call-update
  11.0 0.0 all-gather.7.cloned.1.call-start
  11.0 0.5 all-gather.7.cloned.1.call-update
  11.6 0.7 compare_and_fusion.1
  12.3 86.6 %all-gather.11.cloned.1.call-done = bf16[128,4096]{0,1:T(8,128)(2,1)} async-done(((bf16[128,128]{0,1:T(8,128)(2,1)}), bf16[128,4096]{0,1:T(8,128)(2,1)}) %all-gather.11.cloned.1.call-update) | async-done | bytes 1048592 | tf_op jit(solution)/shard_map/all_gather | solution.py:42
  98.9 1.5 copy.60
  100.3 0.6 gather_fusion.7
  101.0 1.1 broadcast_select_fusion.3
  102.1 7.5 %all-to-all-start.3 = ((bf16[16,128,256]{2,1,0:T(8,128)(2,1)}), bf16[16,128,256]{2,1,0:T(8,128)(2,1)}, u32[]{:S(2)}, u32[]{:S(2)}) async-start(bf16[16,128,256]{2,1,0:T(8,128)(2,1)} %broadcast_select_fusion.3), calls=%async_computation.3 | async-start | bytes 2097152 | tf_op jit(solution)/shard_map/all_to_all | solution.py:96
  109.8 0.5 broadcast_compare_fusion
  110.3 0.5 broadcast_compare_fusion.1
  110.8 72.0 %all-gather.5.cloned.1.call-done = bf16[128,4096]{0,1:T(8,128)(2,1)} async-done(((bf16[128,128]{0,1:T(8,128)(2,1)}), bf16[128,4096]{0,1:T(8,128)(2,1)}) %all-gather.5.cloned.1.call-update) | async-done | bytes 1048592 | tf_op jit(solution)/shard_map/all_gather | solution.py:41
  182.8 1.5 copy.53
  184.2 1.6 gather_fusion.4
  185.8 1.6 copy.65
  187.5 1.1 broadcast_select_fusion.1
  188.6 7.5 %all-to-all-start = ((bf16[16,128,256]{1,2,0:T(8,128)(2,1)}), bf16[16,128,256]{1,2,0:T(8,128)(2,1)}, u32[]{:S(2)}, u32[]{:S(2)}) async-start(bf16[16,128,256]{1,2,0:T(8,128)(2,1)} %broadcast_select_fusion.1), calls=%async_computation | async-start | bytes 2097152 | tf_op jit(solution)/shard_map/all_to_all | solution.py:93
  196.2 0.6 gather_fusion.2
  196.8 0.6 gather_fusion
  197.4 76.1 %all-gather.9.cloned.1.call-done = bf16[1,16,256,256]{3,2,0,1:T(8,128)(2,1)} async-done(((bf16[1,1,256,256]{3,2,0,1:T(8,128)(2,1)}), bf16[1,16,256,256]{3,2,0,1:T(8,128)(2,1)}) %all-gather.9.cloned.1.call-update) | async-done | bytes 2097168 | tf_op jit(solution)/shard_map/all_gather | solution.py:64
  273.5 2.4 fusion.25
  275.9 2.0 fusion.10
  277.9 69.6 %all-gather.7.cloned.1.call-done = bf16[1,16,256,256]{3,2,0,1:T(8,128)(2,1)} async-done(((bf16[1,1,256,256]{3,2,0,1:T(8,128)(2,1)}), bf16[1,16,256,256]{3,2,0,1:T(8,128)(2,1)}) %all-gather.7.cloned.1.call-update) | async-done | bytes 2097168 | tf_op jit(solution)/shard_map/all_gather | solution.py:52
  347.5 2.1 fusion.16
  349.7 2.0 fusion.14
  351.6 0.1 multiply_convert_fusion
  351.8 0.6 gather_fusion.6
  352.4 0.7 copy.70
  353.1 1.2 broadcast_select_fusion
  354.3 4.7 all-to-all-start.2
  359.0 0.2 reduce-scatter.7.cloned.1.call-start
  359.2 0.1 fusion.62
  359.3 0.6 gather_fusion.1
  360.0 0.5 fusion.22
  360.5 0.1 copy-done.5
  360.6 2.3 fusion.37
  362.9 1.7 copy.76
  364.7 0.0 reduce-scatter.7.cloned.1.call-update
  364.7 1.6 gather_fusion.3
  366.3 0.6 gather_fusion.5
  367.0 1.2 broadcast_select_fusion.2
  368.1 0.5 copy-done.3
  368.7 2.2 fusion.19
  370.9 8.0 %all-to-all-done.2 = bf16[16,128,256]{1,2,0:T(8,128)(2,1)} async-done(((bf16[16,128,256]{1,2,0:T(8,128)(2,1)}), bf16[16,128,256]{1,2,0:T(8,128)(2,1)}, u32[]{:S(2)}, u32[]{:S(2)}) %all-to-all-start.2) | async-done | bytes 1048608 | tf_op jit(solution)/shard_map/all_to_all | solution.py:95
  378.8 4.3 all-to-all-start.1
  383.2 0.0 reduce-scatter.9.cloned.1.call-start
  383.3 2.3 fusion.34
  385.6 1.8 copy.77
  387.3 0.0 reduce-scatter.9.cloned.1.call-update
  387.4 0.6 constant_dynamic-slice_fusion.1
  388.0 0.6 constant_dynamic-slice_fusion
  388.6 100.4 %reduce-scatter.7.cloned.1.call-done = bf16[128,128]{1,0:T(8,128)(2,1)} async-done(((bf16[4096,128]{1,0:T(8,128)(2,1)}), bf16[128,128]{1,0:T(8,128)(2,1)}) %reduce-scatter.7.cloned.1.call-update) | async-done | bytes 32784
  489.0 1.5 copy.73
  490.5 125.7 %reduce-scatter.9.cloned.1.call-done = bf16[128,128]{1,0:T(8,128)(2,1)} async-done(((bf16[4096,128]{1,0:T(8,128)(2,1)}), bf16[128,128]{1,0:T(8,128)(2,1)}) %reduce-scatter.9.cloned.1.call-update) | async-done | bytes 32784
  616.2 1.5 copy.75
  617.6 3.3 fusion.45
  620.9 3.2 fusion.44
  (42 shorter events, 0.1 us)
Async XLA Ops:
  7.2 91.7 %all-gather.11.cloned.1.call-start = ((), (), s32[]{:S(2)}) async-start(), calls=%async_computation.9 | async-start | bytes 1081344 | tf_op jit(solution)/shard_map/all_gather | solution.py:42
  8.7 174.0 %all-gather.5.cloned.1.call-start = ((), (), s32[]{:S(2)}) async-start(), calls=%async_computation.6 | async-start | bytes 1081344 | tf_op jit(solution)/shard_map/all_gather | solution.py:41
  10.3 263.2 %all-gather.9.cloned.1.call-start = ((), (), s32[]{:S(2)}) async-start(), calls=%async_computation.8 | async-start | bytes 2228224 | tf_op jit(solution)/shard_map/all_gather | solution.py:64
  11.0 336.5 %all-gather.7.cloned.1.call-start = ((), (), s32[]{:S(2)}) async-start(), calls=%async_computation.7 | async-start | bytes 2228224 | tf_op jit(solution)/shard_map/all_gather | solution.py:52
  12.2 88.7 %copy-start.4 = (s32[16]{0:T(128)}, s32[16]{0:T(128)S(1)}, u32[]{:S(2)}) copy-start(s32[16]{0:T(128)S(1)} %get-tuple-element.11) | copy-start | bytes 196
  101.0 8.7 %copy-start.12 = (s32[1,16]{1,0:T(1,128)S(1)}, s32[1,16]{1,0:T(1,128)}, u32[]{:S(2)}) copy-start(s32[1,16]{1,0:T(1,128)} %param.17) | copy-start | bytes 196
  101.0 9.3 %copy-start.13 = (s32[1,16]{1,0:T(1,128)S(1)}, s32[1,16]{1,0:T(1,128)}, u32[]{:S(2)}) copy-start(s32[1,16]{1,0:T(1,128)} %param.19) | copy-start | bytes 196
  102.1 86.5 %all-to-all-start.3 = ((bf16[16,128,256]{2,1,0:T(8,128)(2,1)}), bf16[16,128,256]{2,1,0:T(8,128)(2,1)}, u32[]{:S(2)}, u32[]{:S(2)}) async-start(bf16[16,128,256]{2,1,0:T(8,128)(2,1)} %broadcast_select_fusion.3), calls=%async_computation.3 | async-start | bytes 2097152 | tf_op jit(solution)/shard_map/all_to_all | solution.py:96
  109.7 239.9 %copy-start.10 = (s32[16]{0:T(128)}, s32[16]{0:T(128)S(1)}, u32[]{:S(2)}) copy-start(s32[16]{0:T(128)S(1)} %get-tuple-element.9) | copy-start | bytes 196
  110.3 239.4 %copy-start.6 = (pred[16]{0:T(512)(128)(4,1)}, pred[16]{0:T(512)(128)(4,1)S(1)}, u32[]{:S(2)}) copy-start(pred[16]{0:T(512)(128)(4,1)S(1)} %get-tuple-element.23) | copy-start | bytes 52
  110.8 165.1 %copy-start.8 = (pred[16]{0:T(512)(128)(4,1)}, pred[16]{0:T(512)(128)(4,1)S(1)}, u32[]{:S(2)}) copy-start(pred[16]{0:T(512)(128)(4,1)S(1)} %get-tuple-element.21) | copy-start | bytes 52
  188.6 165.7 %all-to-all-start = ((bf16[16,128,256]{1,2,0:T(8,128)(2,1)}), bf16[16,128,256]{1,2,0:T(8,128)(2,1)}, u32[]{:S(2)}, u32[]{:S(2)}) async-start(bf16[16,128,256]{1,2,0:T(8,128)(2,1)} %broadcast_select_fusion.1), calls=%async_computation | async-start | bytes 2097152 | tf_op jit(solution)/shard_map/all_to_all | solution.py:93
  354.3 5.7 copy-start.1
  354.3 24.5 %all-to-all-start.2 = ((bf16[16,128,256]{1,2,0:T(8,128)(2,1)}), bf16[16,128,256]{1,2,0:T(8,128)(2,1)}, u32[]{:S(2)}, u32[]{:S(2)}) async-start(bf16[16,128,256]{1,2,0:T(8,128)(2,1)} %broadcast_select_fusion), calls=%async_computation.2 | async-start | bytes 2097152 | tf_op jit(solution)/shard_map/all_to_all | solution.py:95
  359.0 130.0 %reduce-scatter.7.cloned.1.call-start = ((), (), s32[]{:S(2)}) async-start(), calls=%async_computation.10 | async-start | bytes 1081344
  360.0 0.7 copy-start.5
  360.0 0.6 copy-start.9
  362.9 1.8 copy-start.11
  366.3 1.8 copy-start
  366.9 1.7 copy-start.3
  368.6 14.6 %copy-start.7 = (pred[16]{0:T(512)(128)(4,1)S(1)}, pred[16]{0:T(512)(128)(4,1)}, u32[]{:S(2)}) copy-start(pred[16]{0:T(512)(128)(4,1)} %copy-done.6) | copy-start | bytes 52
  370.9 12.4 %copy-start.2 = (f32[128,16,256]{2,0,1:T(8,128)S(1)}, f32[128,16,256]{2,0,1:T(8,128)}, u32[]{:S(2)}) copy-start(f32[128,16,256]{2,0,1:T(8,128)} %fusion.19) | copy-start | bytes 6291460
  378.8 242.1 %all-to-all-start.1 = ((bf16[16,128,256]{2,1,0:T(8,128)(2,1)}), bf16[16,128,256]{2,1,0:T(8,128)(2,1)}, u32[]{:S(2)}, u32[]{:S(2)}) async-start(bf16[16,128,256]{2,1,0:T(8,128)(2,1)} %broadcast_select_fusion.2), calls=%async_computation.1 | async-start | bytes 2097152 | tf_op jit(solution)/shard_map/all_to_all | solution.py:94
  383.2 233.0 %reduce-scatter.9.cloned.1.call-start = ((), (), s32[]{:S(2)}) async-start(), calls=%async_computation.11 | async-start | bytes 1081344
  385.6 1.8 copy-start.14
  385.6 2.4 copy-start.15
Sparse Core Ops, SparseCore 0:
  11.9 86.8 all-gather.10
  102.8 79.9 all-gather.4
  184.8 88.6 all-gather.8
  275.4 72.0 all-gather.6
  364.8 124.1 reduce-scatter.6
  494.2 121.9 reduce-scatter.8
where the time goes:
time: 632 us; the launch traced here: 631 us
  waiting for transfers between devices  540 us (85%)
  starting transfers between devices  24.5 us (4%)
  local copies, waits for them, and re-layouts  23.4 us (4%)
  matrix products  22.3 us (4%)
  between operations  14.5 us (2%)
  other arithmetic  6.7 us (1%)
    unnamed x8, waiting for transfers between devices  227 us
    all_gather x1, waiting for transfers between devices, per_device(): lax.all_gather(upstream, 'col', axis=1, tiled=True)  86.6 us
    all_gather x1, waiting for transfers between devices, per_device(): lax.all_gather(w_out, 'row', axis=1, tiled=True)[0]  76.1 us
    all_gather x1, waiting for transfers between devices, per_device(): lax.all_gather(tokens, 'col', axis=1, tiled=True)  72 us
    all_gather x1, waiting for transfers between devices, per_device(): lax.all_gather(w_in, 'row', axis=1, tiled=True)[0]  69.6 us
  transfers between devices with their start and end apart: 10, of which 7 were waited for; matrix products, arithmetic and copies ran while one was open for 7% of the time, Pallas kernels for 0%

commit v1 on v0

--- a/solution.py
+++ b/solution.py
@@ -38,7 +38,15 @@
     out_row, out_col, out_filled = split_codes(out_codes[0], tile_cols)
     first_slot = lax.axis_index("row") * own_slots
     whole_tokens, whole_upstream = (
-        lax.all_gather(tokens, "col", axis=1, tiled=True),
+        jnp.concatenate(
+            lax.all_to_all(
+                jnp.stack([tokens for _ in range(lax.axis_size("col"))]),
+                axis_name="col",
+                concat_axis=0,
+                split_axis=0,
+            ),
+            axis=1,
+        ),
         lax.all_gather(upstream, "col", axis=1, tiled=True),
     )
     token_tiles = whole_tokens.reshape(row_count, tile_rows, tile_size)

time: 632 us -> 555 us (0.88)
  waiting for transfers between devices: 540 us -> 447 us
  starting transfers between devices: 24.5 us -> 42.9 us
    all_gather x1 -> x0, waiting for transfers between devices: 72 us -> none  [per_device(): lax.all_gather(tokens, 'col', axis=1, tiled=True)]
    all_gather x1, waiting for transfers between devices: 86.6 us -> 37.2 us  [per_device(): lax.all_gather(upstream, 'col', axis=1, tiled=True)]
    all_to_all x0 -> x1, waiting for transfers between devices: none -> 28.2 us  [per_device(): lax.all_to_all(jnp.stack([tokens for _ in range(lax.axis_size('col'))]),...]
    all_to_all x0 -> x1, starting transfers between devices: none -> 10.1 us  [per_device(): lax.all_to_all(jnp.stack([tokens for _ in range(lax.axis_size('col'))]),...]
    unnamed x8 -> x7, waiting for transfers between devices: 227 us -> 227 us
  transfers between devices with their start and end apart: 10 -> 10, of which waited for: 7 -> 7; matrix products, arithmetic and copies ran while one was open for 7% -> 8% of each run, Pallas kernels for 0% -> 0%
where the time goes in v1:
time: 555 us; the launch traced here: 554 us
  waiting for transfers between devices  447 us (81%)
  starting transfers between devices  42.9 us (8%)
  matrix products  22.3 us (4%)
  local copies, waits for them, and re-layouts  21.2 us (4%)
  between operations  14.2 us (3%)
  other arithmetic  6.03 us (1%)
    unnamed x7, waiting for transfers between devices  227 us
    all_gather x1, waiting for transfers between devices, per_device(): lax.all_gather(w_out, 'row', axis=1, tiled=True)[0]  76.7 us
    all_gather x1, waiting for transfers between devices, per_device(): lax.all_gather(w_in, 'row', axis=1, tiled=True)[0]  69.6 us
    all_gather x1, waiting for transfers between devices, per_device(): lax.all_gather(upstream, 'col', axis=1, tiled=True)  37.2 us
    all_to_all x1, waiting for transfers between devices, per_device(): lax.all_to_all(jnp.stack([tokens for _ in range(lax.axis_size('col'))]),...  28.2 us
    all_to_all x1, starting transfers between devices, per_device(): lax.all_to_all(upstream_sends, 'row', split_axis=0, concat_axis=1, tiled=...  12.8 us
  transfers between devices with their start and end apart: 10, of which 7 were waited for; matrix products, arithmetic and copies ran while one was open for 8% of the time, Pallas kernels for 0%

profile of v1, /device:TPU:16, one launch (start us, length us, event | category | flops | bytes accessed | tf_op | source)
XLA Modules:
  0.0 553.8 jit_solution(8638579956523846494)
XLA Ops:
  7.2 0.0 all-gather.8.cloned.1.call-start
  7.2 1.5 copy.62
  8.7 0.0 all-gather.8.cloned.1.call-update
  8.7 0.0 all-gather.6.cloned.1.call-start
  8.8 0.7 all-gather.6.cloned.1.call-update
  9.5 0.9 copy.55
  10.3 1.3 stack.2
  11.6 10.1 %all-to-all-start = ((bf16[32,128,128]{1,2,0:T(8,128)(2,1)}), bf16[32,128,128]{1,2,0:T(8,128)(2,1)S(1)}, u32[]{:S(2)}, u32[]{:S(2)}) async-start(bf16[32,128,128]{1,2,0:T(8,128)(2,1)} %stack.2), calls=%async_computation | async-start | bytes 2097152 | tf_op jit(solution)/shard_map/all_to_all | solution.py:42
  21.7 0.0 all-gather.4.cloned.1.call-start
  21.7 0.7 all-gather.4.cloned.1.call-update
  22.5 28.2 %all-to-all-done = bf16[32,128,128]{1,2,0:T(8,128)(2,1)S(1)} async-done(((bf16[32,128,128]{1,2,0:T(8,128)(2,1)}), bf16[32,128,128]{1,2,0:T(8,128)(2,1)S(1)}, u32[]{:S(2)}, u32[]{:S(2)}) %all-to-all-start) | async-done | bytes 1048608 | tf_op jit(solution)/shard_map/all_to_all | solution.py:42
  50.7 0.5 copy.56
  51.2 0.6 gather_fusion.4
  51.8 0.7 copy.68
  52.5 0.0 copy-start.13
  52.5 1.1 broadcast_select_fusion.1
  53.6 10.7 %all-to-all-start.1 = ((bf16[16,128,256]{1,2,0:T(8,128)(2,1)}), bf16[16,128,256]{1,2,0:T(8,128)(2,1)}, u32[]{:S(2)}, u32[]{:S(2)}) async-start(bf16[16,128,256]{1,2,0:T(8,128)(2,1)} %broadcast_select_fusion.1), calls=%async_computation.1 | async-start | bytes 2097152 | tf_op jit(solution)/shard_map/all_to_all | solution.py:101
  64.5 0.5 broadcast_compare_fusion
  65.0 0.5 broadcast_compare_fusion.1
  65.5 37.2 %all-gather.8.cloned.1.call-done = bf16[128,4096]{0,1:T(8,128)(2,1)} async-done(((bf16[128,128]{0,1:T(8,128)(2,1)}), bf16[128,4096]{0,1:T(8,128)(2,1)}) %all-gather.8.cloned.1.call-update) | async-done | bytes 1048592 | tf_op jit(solution)/shard_map/all_gather | solution.py:50
  102.6 1.5 copy.63
  104.1 0.6 gather_fusion.7
  104.8 1.1 broadcast_select_fusion.3
  105.9 12.8 %all-to-all-start.4 = ((bf16[16,128,256]{2,1,0:T(8,128)(2,1)}), bf16[16,128,256]{2,1,0:T(8,128)(2,1)}, u32[]{:S(2)}, u32[]{:S(2)}) async-start(bf16[16,128,256]{2,1,0:T(8,128)(2,1)} %broadcast_select_fusion.3), calls=%async_computation.4 | async-start | bytes 2097152 | tf_op jit(solution)/shard_map/all_to_all | solution.py:104
  118.7 0.6 gather_fusion
  119.3 0.6 gather_fusion.2
  119.9 76.7 %all-gather.6.cloned.1.call-done = bf16[1,16,256,256]{3,2,0,1:T(8,128)(2,1)} async-done(((bf16[1,1,256,256]{3,2,0,1:T(8,128)(2,1)}), bf16[1,16,256,256]{3,2,0,1:T(8,128)(2,1)}) %all-gather.6.cloned.1.call-update) | async-done | bytes 2097168 | tf_op jit(solution)/shard_map/all_gather | solution.py:72
  196.7 2.4 fusion.25
  199.1 2.0 fusion.10
  201.1 69.6 %all-gather.4.cloned.1.call-done = bf16[1,16,256,256]{3,2,0,1:T(8,128)(2,1)} async-done(((bf16[1,1,256,256]{3,2,0,1:T(8,128)(2,1)}), bf16[1,16,256,256]{3,2,0,1:T(8,128)(2,1)}) %all-gather.4.cloned.1.call-update) | async-done | bytes 2097168 | tf_op jit(solution)/shard_map/all_gather | solution.py:60
  270.7 2.1 fusion.16
  272.8 2.0 fusion.14
  274.8 0.1 multiply_convert_fusion
  275.0 0.6 gather_fusion.6
  275.6 0.7 copy.73
  276.2 1.3 broadcast_select_fusion
  277.5 4.7 all-to-all-start.3
  282.2 0.2 reduce-scatter.7.cloned.1.call-start
  282.4 0.1 fusion.62
  282.5 0.6 gather_fusion.1
  283.2 0.5 fusion.22
  283.7 0.1 copy-done.5
  283.8 2.3 fusion.37
  286.1 1.7 copy.79
  287.9 0.0 reduce-scatter.7.cloned.1.call-update
  287.9 1.6 gather_fusion.3
  289.5 0.6 gather_fusion.5
  290.1 1.2 broadcast_select_fusion.2
  291.3 0.5 copy-done.3
  291.8 2.2 fusion.19
  294.1 8.0 %all-to-all-done.3 = bf16[16,128,256]{1,2,0:T(8,128)(2,1)} async-done(((bf16[16,128,256]{1,2,0:T(8,128)(2,1)}), bf16[16,128,256]{1,2,0:T(8,128)(2,1)}, u32[]{:S(2)}, u32[]{:S(2)}) %all-to-all-start.3) | async-done | bytes 1048608 | tf_op jit(solution)/shard_map/all_to_all | solution.py:103
  302.0 4.3 all-to-all-start.2
  306.4 0.0 reduce-scatter.9.cloned.1.call-start
  306.4 2.3 fusion.34
  308.8 1.7 copy.80
  310.5 0.0 reduce-scatter.9.cloned.1.call-update
  310.6 0.6 constant_dynamic-slice_fusion.1
  311.2 0.6 constant_dynamic-slice_fusion
  311.8 100.5 %reduce-scatter.7.cloned.1.call-done = bf16[128,128]{1,0:T(8,128)(2,1)} async-done(((bf16[4096,128]{1,0:T(8,128)(2,1)}), bf16[128,128]{1,0:T(8,128)(2,1)}) %reduce-scatter.7.cloned.1.call-update) | async-done | bytes 32784
  412.2 1.5 copy.76
  413.7 125.5 %reduce-scatter.9.cloned.1.call-done = bf16[128,128]{1,0:T(8,128)(2,1)} async-done(((bf16[4096,128]{1,0:T(8,128)(2,1)}), bf16[128,128]{1,0:T(8,128)(2,1)}) %reduce-scatter.9.cloned.1.call-update) | async-done | bytes 32784
  539.2 1.5 copy.78
  540.7 3.3 fusion.45
  544.0 3.3 fusion.44
  (42 shorter events, 0.1 us)
Async XLA Ops:
  7.2 15.2 %copy-start.12 = (s32[1,16]{1,0:T(1,128)S(1)}, s32[1,16]{1,0:T(1,128)}, u32[]{:S(2)}) copy-start(s32[1,16]{1,0:T(1,128)} %param.17) | copy-start | bytes 196
  7.2 95.5 %all-gather.8.cloned.1.call-start = ((), (), s32[]{:S(2)}) async-start(), calls=%async_computation.9 | async-start | bytes 1081344 | tf_op jit(solution)/shard_map/all_gather | solution.py:50
  8.7 188.0 %all-gather.6.cloned.1.call-start = ((), (), s32[]{:S(2)}) async-start(), calls=%async_computation.8 | async-start | bytes 2228224 | tf_op jit(solution)/shard_map/all_gather | solution.py:72
  11.6 39.1 %all-to-all-start = ((bf16[32,128,128]{1,2,0:T(8,128)(2,1)}), bf16[32,128,128]{1,2,0:T(8,128)(2,1)S(1)}, u32[]{:S(2)}, u32[]{:S(2)}) async-start(bf16[32,128,128]{1,2,0:T(8,128)(2,1)} %stack.2), calls=%async_computation | async-start | bytes 2097152 | tf_op jit(solution)/shard_map/all_to_all | solution.py:42
  21.7 249.1 %all-gather.4.cloned.1.call-start = ((), (), s32[]{:S(2)}) async-start(), calls=%async_computation.7 | async-start | bytes 2228224 | tf_op jit(solution)/shard_map/all_gather | solution.py:60
  22.4 250.4 %copy-start.10 = (s32[16]{0:T(128)}, s32[16]{0:T(128)S(1)}, u32[]{:S(2)}) copy-start(s32[16]{0:T(128)S(1)} %get-tuple-element.9) | copy-start | bytes 196
  52.5 11.9 %copy-start.13 = (s32[1,16]{1,0:T(1,128)S(1)}, s32[1,16]{1,0:T(1,128)}, u32[]{:S(2)}) copy-start(s32[1,16]{1,0:T(1,128)} %param.19) | copy-start | bytes 196
  53.6 52.3 %all-to-all-start.1 = ((bf16[16,128,256]{1,2,0:T(8,128)(2,1)}), bf16[16,128,256]{1,2,0:T(8,128)(2,1)}, u32[]{:S(2)}, u32[]{:S(2)}) async-start(bf16[16,128,256]{1,2,0:T(8,128)(2,1)} %broadcast_select_fusion.1), calls=%async_computation.1 | async-start | bytes 2097152 | tf_op jit(solution)/shard_map/all_to_all | solution.py:101
  64.4 40.3 %copy-start.4 = (s32[16]{0:T(128)}, s32[16]{0:T(128)S(1)}, u32[]{:S(2)}) copy-start(s32[16]{0:T(128)S(1)} %get-tuple-element.11) | copy-start | bytes 196
  65.0 207.9 %copy-start.6 = (pred[16]{0:T(512)(128)(4,1)}, pred[16]{0:T(512)(128)(4,1)S(1)}, u32[]{:S(2)}) copy-start(pred[16]{0:T(512)(128)(4,1)S(1)} %get-tuple-element.23) | copy-start | bytes 52
  65.5 133.6 %copy-start.8 = (pred[16]{0:T(512)(128)(4,1)}, pred[16]{0:T(512)(128)(4,1)S(1)}, u32[]{:S(2)}) copy-start(pred[16]{0:T(512)(128)(4,1)S(1)} %get-tuple-element.21) | copy-start | bytes 52
  105.9 171.6 %all-to-all-start.4 = ((bf16[16,128,256]{2,1,0:T(8,128)(2,1)}), bf16[16,128,256]{2,1,0:T(8,128)(2,1)}, u32[]{:S(2)}, u32[]{:S(2)}) async-start(bf16[16,128,256]{2,1,0:T(8,128)(2,1)} %broadcast_select_fusion.3), calls=%async_computation.4 | async-start | bytes 2097152 | tf_op jit(solution)/shard_map/all_to_all | solution.py:104
  277.5 5.7 %copy-start.1 = (bf16[1,16,256,256]{3,2,0,1:T(8,128)(2,1)S(1)}, bf16[1,16,256,256]{3,2,0,1:T(8,128)(2,1)}, u32[]{:S(2)}) copy-start(bf16[1,16,256,256]{3,2,0,1:T(8,128)(2,1)} %all-gather.6.cloned.1.call-done) | copy-start | bytes 6291460
  277.5 24.5 %all-to-all-start.3 = ((bf16[16,128,256]{1,2,0:T(8,128)(2,1)}), bf16[16,128,256]{1,2,0:T(8,128)(2,1)}, u32[]{:S(2)}, u32[]{:S(2)}) async-start(bf16[16,128,256]{1,2,0:T(8,128)(2,1)} %broadcast_select_fusion), calls=%async_computation.3 | async-start | bytes 2097152 | tf_op jit(solution)/shard_map/all_to_all | solution.py:103
  282.2 130.1 %reduce-scatter.7.cloned.1.call-start = ((), (), s32[]{:S(2)}) async-start(), calls=%async_computation.10 | async-start | bytes 1081344
  283.2 0.7 copy-start.5
  283.2 0.6 copy-start.9
  286.1 1.8 copy-start.11
  289.5 1.8 copy-start
  290.1 1.7 copy-start.3
  291.8 14.6 %copy-start.7 = (pred[16]{0:T(512)(128)(4,1)S(1)}, pred[16]{0:T(512)(128)(4,1)}, u32[]{:S(2)}) copy-start(pred[16]{0:T(512)(128)(4,1)} %copy-done.6) | copy-start | bytes 52
  294.1 12.4 %copy-start.2 = (f32[128,16,256]{2,0,1:T(8,128)S(1)}, f32[128,16,256]{2,0,1:T(8,128)}, u32[]{:S(2)}) copy-start(f32[128,16,256]{2,0,1:T(8,128)} %fusion.19) | copy-start | bytes 6291460
  302.0 242.0 %all-to-all-start.2 = ((bf16[16,128,256]{2,1,0:T(8,128)(2,1)}), bf16[16,128,256]{2,1,0:T(8,128)(2,1)}, u32[]{:S(2)}, u32[]{:S(2)}) async-start(bf16[16,128,256]{2,1,0:T(8,128)(2,1)} %broadcast_select_fusion.2), calls=%async_computation.2 | async-start | bytes 2097152 | tf_op jit(solution)/shard_map/all_to_all | solution.py:102
  306.4 232.9 %reduce-scatter.9.cloned.1.call-start = ((), (), s32[]{:S(2)}) async-start(), calls=%async_computation.11 | async-start | bytes 1081344
  308.8 1.8 copy-start.14
  308.8 2.4 copy-start.15
Sparse Core Ops, SparseCore 0:
  11.9 90.6 all-gather.7
  104.7 91.9 all-gather.5
  198.8 71.9 all-gather.3
  288.0 124.1 reduce-scatter.6
  417.4 121.7 reduce-scatter.8
